TPU v7x, 32 devices: a whole 2x2x4 slice. The times are simulated.
32 devices in a mesh: ka: 4 (over y, x), hist: 8 (over z, core).
Axes of the slice: x: 2, y: 2, z: 4, core: 2. Of those that a mesh axis runs over, the one named last changes fastest.
Arguments:
- step_index: int32 [1], replicated, may hold values from 9 to 32
- band_energy: float32 [32, 3, 512], P('hist', None, 'ka'), may hold values from -1 to 3
- kernel_row: bfloat16 [32, 2, 3, 3, 512], P('hist', None, None, None, 'ka'), may hold values from -0.5 to 0.5
- lattice_history: bfloat16 [32, 2, 3, 3, 32, 512], P('hist', None, None, None, None, 'ka'), may hold values from -6 to 6, as said below
- diagonal_inverse: float32 [2, 3, 3, 512], P(None, None, None, 'ka'), may hold values from -3 to 3
- multiplicity: int32 [512], P('ka'), may hold values from 1 to 32, as said below
- state_energy: float32 [64], replicated, may hold values from -3 to 3
- connection: int32 [64, 6], replicated, may hold values from 0 to 63, as said below
- predicted_row: float32 [2, 64, 32], P(None, None, 'hist'), may hold values from -6 to 6
- pseudo_history: bfloat16 [32, 2, 64, 32], P('hist'), may hold values from -6 to 6, as said below
Outputs:
- lattice_row: bfloat16 [32, 2, 3, 3, 512], P('hist', None, None, None, 'ka')
- local_row: float32 [2, 3, 3, 32], P(None, None, None, 'hist')
- pseudo_row: float32 [2, 64, 32], P(None, None, 'hist')
Inputs may be any that keep to these rules, and one draw needn't show every extreme that they name: `lattice_history`: the stored lattice propagators vanish where the column time j exceeds the row time m. `pseudo_history`: the stored pseudo-particle propagators vanish where the column time j exceeds the row time m. `multiplicity`: powers of two. For each flavour f, s -> connection[s, f] is an involution without fixed points; two states that flavour f links differ in that flavour's occupation, under a numbering of the states drawn from the seed.
All inputs are finite; a program needn't handle non-finite values.
Results may differ from a plain program's by a relative error of at most 0.012.
Values may be sent and summed in bfloat16 or wider, within the bound.
A program may use at most 64 MiB of HBM per device.

v0:
```python
import jax
import jax.numpy as jnp
from jax import lax
from jax.sharding import PartitionSpec as P

time_step = 0.05
coupling = 0.02


def entering(part, axis, combine, identity):
    place = lax.axis_index(axis)
    gathered = lax.all_gather(part, axis)
    state = jnp.zeros_like(part) + jnp.asarray(identity, part.dtype)

    def one(hop, state):
        return combine(state, lax.dynamic_index_in_dim(gathered, hop, 0, False))

    return lax.fori_loop(0, place, one, state)


def complex_form(kernel):
    part_real = kernel[:, 0]
    part_imag = kernel[:, 1]
    upper = jnp.stack([part_real, -part_imag], axis=2)
    lower_half = jnp.stack([part_imag, part_real], axis=2)
    return jnp.stack([upper, lower_half], axis=1)


def contract(matrix, vector):
    return jnp.einsum("abk,jbck->jack", matrix, vector, precision=lax.Precision.HIGHEST)


def add_terms(earlier, later):
    return earlier + later


def per_device(
    step_index,
    band_energy,
    kernel_row,
    lattice_history,
    diagonal_inverse,
    multiplicity,
    state_energy,
    connection,
    predicted_row,
    pseudo_history,
):
    current = step_index[0]
    block_len = band_energy.shape[0]
    position = lax.axis_index("hist")
    owned_times = position * block_len + jnp.arange(block_len, dtype=jnp.int32)
    before_now = (owned_times < current).astype(jnp.float32)
    weight = jnp.where(owned_times == 0, 0.5, 1.0).astype(jnp.float32) * before_now
    in_range = (owned_times <= current).astype(jnp.float32)
    angles = None
    block_sum = jnp.sum(band_energy, axis=0)
    masked_sum = jnp.sum(band_energy * before_now[:, None, None], axis=0)
    earlier_blocks = entering(block_sum, "hist", add_terms, jnp.zeros_like(block_sum))
    upto_now = lax.psum(masked_sum, "hist")
    earlier = jnp.cumsum(band_energy, axis=0) - band_energy
    angles = time_step * (upto_now[None] - earlier_blocks[None] - earlier)
    kernel = kernel_row * weight.astype(jnp.bfloat16)[:, None, None, None, None]
    columns = lax.all_to_all(lattice_history, "hist", split_axis=4, concat_axis=0, tiled=True)
    full_kernel = lax.all_gather(kernel, "hist", axis=0, tiled=True)
    volterra_terms = jnp.einsum(
        "msapbk,mpbcjk->jsack",
        complex_form(full_kernel),
        columns,
        preferred_element_type=jnp.float32,
    )
    free_pair = (
        jnp.stack([-jnp.sin(angles), -jnp.cos(angles)], axis=1) * in_range[:, None, None, None]
    )
    identity = jnp.eye(3, dtype=jnp.float32)
    free_rows = free_pair[:, :, :, None, :] * identity[None, None, :, :, None]
    right_side = volterra_terms + free_rows
    out_real = contract(diagonal_inverse[0], right_side[:, 0]) - contract(
        diagonal_inverse[1], right_side[:, 1]
    )
    out_imag = contract(diagonal_inverse[0], right_side[:, 1]) + contract(
        diagonal_inverse[1], right_side[:, 0]
    )
    fresh_rows = jnp.stack([out_real, out_imag], axis=1)
    lattice_row = fresh_rows.astype(jnp.bfloat16)
    weights_k = multiplicity.astype(jnp.float32)
    weighted = jnp.einsum("jsack,k->jsac", fresh_rows, weights_k, precision=lax.Precision.HIGHEST)
    summed, total_mult = lax.psum((weighted, jnp.sum(weights_k)), "ka")
    local_rows = jnp.transpose(summed / total_mult, (1, 2, 3, 0))
    hybrid = jnp.repeat(jnp.diagonal(local_rows, axis1=1, axis2=2), 2, axis=2)
    hyb_real = hybrid[0].T
    hyb_imag = hybrid[1].T
    onehot = (
        connection[:, :, None] == jnp.arange(connection.shape[0], dtype=jnp.int32)[None, None, :]
    ).astype(jnp.float32)
    reached = jnp.einsum("sft,ptm->psfm", onehot, predicted_row, precision=lax.Precision.HIGHEST)
    self_real = coupling * jnp.sum(
        hyb_real[None] * reached[0] - hyb_imag[None] * reached[1], axis=1
    )
    self_imag = coupling * jnp.sum(
        hyb_real[None] * reached[1] + hyb_imag[None] * reached[0], axis=1
    )
    wself_real = (self_real * weight[None, :]).T
    wself_imag = (self_imag * weight[None, :]).T
    hist_real = pseudo_history[:, 0].astype(jnp.float32)
    hist_imag = pseudo_history[:, 1].astype(jnp.float32)
    sum_real = jnp.sum(
        wself_real[:, :, None] * hist_real - wself_imag[:, :, None] * hist_imag, axis=0
    )
    sum_imag = jnp.sum(
        wself_real[:, :, None] * hist_imag + wself_imag[:, :, None] * hist_real, axis=0
    )
    shares = lax.psum_scatter(
        jnp.stack([sum_real, sum_imag], axis=0).astype(jnp.bfloat16),
        "hist",
        scatter_dimension=2,
        tiled=True,
    ).astype(jnp.float32)
    elapsed = (current - owned_times).astype(jnp.float32)
    spins = state_energy[:, None] * time_step * elapsed[None, :]
    free_pseudo = jnp.stack([-jnp.sin(spins), -jnp.cos(spins)], axis=0) * in_range[None, None, :]
    return (lattice_row, local_rows, free_pseudo + shares)


def solution(mesh):
    in_specs = (
        P(),
        P("hist", None, "ka"),
        P("hist", None, None, None, "ka"),
        P("hist", None, None, None, None, "ka"),
        P(None, None, None, "ka"),
        P("ka"),
        P(),
        P(),
        P(None, None, "hist"),
        P("hist", None, None, None),
    )
    out_specs = (
        P("hist", None, None, None, "ka"),
        P(None, None, None, "hist"),
        P(None, None, "hist"),
    )
    return jax.shard_map(
        per_device, mesh=mesh, in_specs=in_specs, out_specs=out_specs, check_vma=False
    )
```

profile of v0, /device:TPU:0, one launch (start us, length us, event | category | flops | bytes accessed | tf_op | source)
XLA Modules:
  0.0 130.3 jit_solution(1153776522976633198)
XLA Ops:
  0.7 2.3 %copy.96 = bf16[4,2,3,3,32,128]{5,0,3,2,1,4:T(4,128)(2,1)} copy(bf16[4,2,3,3,32,128]{5,4,3,2,1,0:T(8,128)(2,1)} %param.15) | data formatting | bytes 1179648 | tf_op args[3]
  3.0 6.5 %all-to-all-start = ((bf16[4,2,3,3,32,128]{5,0,3,2,1,4:T(4,128)(2,1)}), bf16[4,2,3,3,32,128]{5,0,3,2,1,4:T(4,128)(2,1)S(1)}, u32[]{:S(2)}, u32[]{:S(2)}) async-start(bf16[4,2,3,3,32,128]{5,0,3,2,1,4:T(4,128)(2,1)} %copy.96), calls=%async_computation | async-start | bytes 1179648 | tf_op jit(solution)/shard_map/all_to_all | solution.py:64
  10.3 22.2 %all_gather.9 = bf16[32,2,3,3,128]{4,1,3,2,0:T(2,128)(2,1)S(1)} all-gather(bf16[4,2,3,3,128]{4,1,3,2,0:T(2,128)(2,1)S(1)} %broadcast_multiply_fusion), channel_id=1, replica_groups=mesh['ka'=4,'hist'=8] {'hist'}, dimensions={0}, use_global_device_ids=true | all-gather | bytes 165888 | tf_op jit(solution)/shard_map/all_gather | solution.py:65
  32.9 12.8 %all-gather.1 = f32[8,3,128]{2,1,0:T(4,128)S(1)} all-gather(f32[1,3,128]{2,1,0:T(4,128)S(1)} %bitcast.157), channel_id=2, replica_groups=mesh['ka'=4,'hist'=8] {'hist'}, dimensions={0}, use_global_device_ids=true | all-gather | bytes 13824 | tf_op jit(solution)/shard_map/all_gather | solution.py:12
  45.7 15.3 %psum.21 = f32[3,128]{1,0:T(4,128)S(1)} all-reduce(f32[3,128]{1,0:T(4,128)S(1)} %get-tuple-element.47), channel_id=1, replica_groups=mesh['ka'=4,'hist'=8] {'hist'}, use_global_device_ids=true, to_apply=%region_1.2 | all-reduce | flops 384 | bytes 3072 | tf_op jit(solution)/shard_map/psum | solution.py:60
  61.3 2.5 %copy.116 = bf16[32,2,3,2,3,128,1]{0,2,3,4,6,1,5:T(4,128)(2,1)} copy(bf16[32,2,3,2,3,128,1]{5,0,4,3,2,1,6:T(8,128)(2,1)S(1)} %maximum_bitcast_fusion) | data formatting | bytes 589824 | tf_op jit(solution)/shard_map/stack | solution.py:26
  63.8 0.3 copy.100
  64.5 0.6 dynamic-slice
  65.7 0.6 convert_reduce_fusion
  66.5 0.4 convolution_bitcast_fusion
  66.9 0.3 copy.97
  67.2 3.3 %copy.117 = bf16[32,2,3,3,4,128,1]{0,4,1,2,3,6,5:T(4,128)(2,1)} copy(bf16[32,2,3,3,4,128,1]{5,0,4,3,2,1,6:T(8,128)(2,1)S(1)} %bitcast.147) | data formatting | bytes 1179648 | tf_op jit(solution)/shard_map/all_to_all | solution.py:64
  70.5 10.3 %bitcast_add_fusion.1 = f32[4,2,3,3,128]{0,2,3,1,4:T(4,128)S(1)} fusion(bf16[32,2,3,2,3,128,1]{0,2,3,4,6,1,5:T(4,128)(2,1)} %copy.116, bf16[32,2,3,3,4,128,1]{0,4,1,2,3,6,5:T(4,128)(2,1)} %copy.117, f32[3,3]{0,1:T(4,128)S(1)} %fusion.21, f32[4,2,3,128]{0,2,1,3:T(4,128)S(1)} %copy.100), kind=kOutput, calls=%fused_computation.2 | convolution fusion | flops 3557376 | bytes 933924 | tf_op jit(solution)/shard_map/msapbk,mpbcjk->jsack/dot_general | solution.py:66
  80.8 1.9 %fusion.2 = f32[128,4,3,3]{1,3,2,0:T(4,128)S(1)} fusion(f32[4,2,3,3,128]{0,2,3,1,4:T(4,128)S(1)} %bitcast_add_fusion.1, f32[1,3,3,128]{2,1,3,0:T(4,128)S(1)} %copy.138), kind=kOutput, calls=%fused_computation.10 | convolution fusion | flops 165888 | bytes 1067008 | tf_op jit(solution)/shard_map/abk,jbck->jack/dot_general | solution.py:30
  82.7 1.9 %fusion.3 = f32[128,4,3,3]{1,3,2,0:T(4,128)S(1)} fusion(f32[4,2,3,3,128]{0,2,3,1,4:T(4,128)S(1)} %bitcast_add_fusion.1, f32[1,3,3,128]{2,1,3,0:T(4,128)S(1)} %copy.138), kind=kOutput, calls=%fused_computation.11 | convolution fusion | flops 165888 | bytes 1067008 | tf_op jit(solution)/shard_map/abk,jbck->jack/dot_general | solution.py:30
  84.5 1.9 %fusion.1 = f32[4,1,3,3,128]{0,2,3,4,1:T(4,128)S(1)} fusion(f32[128,4,3,3]{1,3,2,0:T(4,128)S(1)} %fusion.2, f32[4,2,3,3,128]{0,2,3,1,4:T(4,128)S(1)} %bitcast_add_fusion.1, f32[1,3,3,128]{2,1,3,0:T(4,128)S(1)} %copy.139), kind=kOutput, calls=%fused_computation.6 | convolution fusion | flops 170496 | bytes 1853440 | tf_op jit(solution)/shard_map/abk,jbck->jack/dot_general | solution.py:30
  86.7 1.9 %fusion = f32[4,1,3,3,128]{0,2,3,4,1:T(4,128)S(1)} fusion(f32[128,4,3,3]{1,3,2,0:T(4,128)S(1)} %fusion.3, f32[4,2,3,3,128]{0,2,3,1,4:T(4,128)S(1)} %bitcast_add_fusion.1, f32[1,3,3,128]{2,1,3,0:T(4,128)S(1)} %copy.139), kind=kOutput, calls=%fused_computation.4 | convolution fusion | flops 170496 | bytes 1853440 | tf_op jit(solution)/shard_map/abk,jbck->jack/dot_general | solution.py:30
  89.4 10.9 %all-reduce.1 = (f32[4,2,3,3]{0,1,3,2:T(2,128)S(1)}, f32[]{:T(128)}) all-reduce(f32[4,2,3,3]{0,1,3,2:T(2,128)S(1)} %bitcast.149, f32[]{:T(128)} %convert_reduce_fusion), channel_id=1, replica_groups=mesh['ka'=4,'hist'=8] {'ka'}, use_global_device_ids=true, to_apply=%region_6.7 | all-reduce | flops 73 | bytes 584 | tf_op jit(solution)/shard_map/psum | solution.py:88
  100.3 0.7 fusion.33
  100.9 1.3 fusion.34
  102.2 0.6 gather_fusion
  103.1 25.9 %all-reduce = bf16[2,64,32]{1,2,0:T(8,128)(2,1)S(1)} all-reduce(bf16[2,64,32]{1,2,0:T(8,128)(2,1)S(1)} %pad_maximum_fusion.2), channel_id=3, replica_groups=mesh['ka'=4,'hist'=8] {'hist'}, use_global_device_ids=true, to_apply=%region_13.14.clone | all-reduce | flops 4096 | bytes 16384
  129.0 0.6 copy.115
  129.6 0.7 fusion.17
  (59 shorter events, 2.4 us)
Async XLA Ops:
  0.6 65.8 %copy-start = (f32[2,64,4]{1,2,0:T(4,128)S(1)}, f32[2,64,4]{1,2,0:T(4,128)}, u32[]{:S(2)}) copy-start(f32[2,64,4]{1,2,0:T(4,128)} %param.20) | copy-start | bytes 6148
  0.6 9.5 %copy-start.3 = (bf16[4,2,3,3,128]{4,1,3,2,0:T(2,128)(2,1)S(1)}, bf16[4,2,3,3,128]{4,1,3,2,0:T(2,128)(2,1)}, u32[]{:S(2)}) copy-start(bf16[4,2,3,3,128]{4,1,3,2,0:T(2,128)(2,1)} %param.14) | copy-start | bytes 55300
  0.7 32.1 %copy-start.2 = (f32[4,3,128]{2,0,1:T(4,128)S(1)}, f32[4,3,128]{2,0,1:T(4,128)}, u32[]{:S(2)}) copy-start(f32[4,3,128]{2,0,1:T(4,128)} %param.13) | copy-start | bytes 18436
  3.0 58.0 %copy-start.4 = (f32[2,3,3,128]{3,0,2,1:T(2,128)S(1)}, f32[2,3,3,128]{3,0,2,1:T(2,128)}, u32[]{:S(2)}) copy-start(f32[2,3,3,128]{3,0,2,1:T(2,128)} %param.16) | copy-start | bytes 27652
  3.0 63.9 %all-to-all-start = ((bf16[4,2,3,3,32,128]{5,0,3,2,1,4:T(4,128)(2,1)}), bf16[4,2,3,3,32,128]{5,0,3,2,1,4:T(4,128)(2,1)S(1)}, u32[]{:S(2)}, u32[]{:S(2)}) async-start(bf16[4,2,3,3,32,128]{5,0,3,2,1,4:T(4,128)(2,1)} %copy.96), calls=%async_computation | async-start | bytes 1179648 | tf_op jit(solution)/shard_map/all_to_all | solution.py:64
  61.1 3.4 %copy-start.8 = (u32[32]{0:T(128)S(1)}, u32[32]{0:T(128)}, u32[]{:S(2)}) copy-start(u32[32]{0:T(128)} %constant.58) | copy-start | bytes 388
  61.1 4.6 %copy-start.5 = (s32[128]{0:T(128)S(1)}, s32[128]{0:T(128)}, u32[]{:S(2)}) copy-start(s32[128]{0:T(128)} %param.17) | copy-start | bytes 1540
  61.1 5.2 %copy-start.7 = (f32[64]{0:T(128)S(1)}, f32[64]{0:T(128)}, u32[]{:S(2)}) copy-start(f32[64]{0:T(128)} %param.18) | copy-start | bytes 772
  61.1 5.3 %copy-start.6 = (s32[64,6]{0,1:T(8,128)S(1)}, s32[64,6]{0,1:T(8,128)}, u32[]{:S(2)}) copy-start(s32[64,6]{0,1:T(8,128)} %param.19) | copy-start | bytes 4612
  86.7 16.3 %copy-start.1 = (bf16[4,2,64,32]{2,3,1,0:T(8,128)(2,1)S(1)}, bf16[4,2,64,32]{2,3,1,0:T(8,128)(2,1)}, u32[]{:S(2)}) copy-start(bf16[4,2,64,32]{2,3,1,0:T(8,128)(2,1)} %param.21) | copy-start | bytes 98308
where the time goes:
time: 131 us; the launch traced here: 130 us
  blocking collectives  87.1 us (66%)
  matrix products  18.5 us (14%)
  local copies, waits for them, and re-layouts  11.9 us (9%)
  starting transfers between devices  6.49 us (5%)
  other arithmetic  3.97 us (3%)
  between operations  2.29 us (2%)
    unnamed x1, blocking collectives  25.9 us
    all_gather x1, blocking collectives, per_device(): full_kernel = lax.all_gather(kernel, 'hist', axis=0, tiled=True)  22.2 us
    psum x1, blocking collectives, per_device(): upto_now = lax.psum(masked_sum, 'hist')  15.3 us
    all_gather x1, blocking collectives, entering(): gathered = lax.all_gather(part, axis)  12.8 us
    psum x1, blocking collectives, per_device(): summed, total_mult = lax.psum((weighted, jnp.sum(weights_k)), 'ka')  10.9 us
    dot_general x1, matrix products, per_device(): jnp.einsum('msapbk,mpbcjk->jsack', complex_form(full_kernel), columns, pr...  10.3 us
    dot_general x4, matrix products, contract(): jnp.einsum('abk,jbck->jack', matrix, vector, precision=lax.Precision.HIGH...  7.6 us
    all_to_all x1, starting transfers between devices, per_device(): lax.all_to_all(lattice_history, 'hist', split_axis=4, concat_axis=0, tile...  6.49 us
  transfers between devices with their start and end apart: 1, of which 0 were waited for; matrix products, arithmetic and copies ran while one was open for 4% of the time, Pallas kernels for 0%

commit v1 on v0

v1 whole, which is shorter than its diff:
```python
import functools

import jax
import jax.numpy as jnp
from jax import lax
from jax.experimental import pallas as pl
from jax.experimental.pallas import tpu as pltpu
from jax.sharding import PartitionSpec as P

time_step = 0.05
coupling = 0.02
tile_rows = 16
highest = lax.Precision.HIGHEST


def dot_rows(left, right, precision=None):
    return lax.dot_general(
        left,
        right,
        (((1,), (1,)), ((), ())),
        precision=precision,
        preferred_element_type=jnp.float32,
    )


def eye(size, dtype):
    rows = lax.broadcasted_iota(jnp.int32, (size, size), 0)
    cols = lax.broadcasted_iota(jnp.int32, (size, size), 1)
    return jnp.where(rows == cols, 1.0, 0.0).astype(dtype)


def kernel(
    n_hist,
    n_ka,
    step_ref,
    band_ref,
    krow_ref,
    hist_ref,
    dinv_ref,
    mult_ref,
    energy_ref,
    conn_ref,
    pred_ref,
    pseudo_ref,
    lattice_out,
    local_out,
    pseudo_out,
    kw,
    stage,
    psend,
    precv,
    drep,
    frep,
    total,
    ksend,
    krecv,
    turned,
    qsend,
    qrecv,
    psend_sem,
    precv_sem,
    ksend_sem,
    krecv_sem,
    qsend_sem,
    qrecv_sem,
):
    block, orb, lanes = band_ref.shape
    times = hist_ref.shape[4]
    states = energy_ref.shape[1]
    pairs = 2 * orb * orb
    rows = pairs * block
    per_tile = tile_rows // block
    me = lax.axis_index("hist")
    my_ka = lax.axis_index("ka")

    barrier = pltpu.get_barrier_semaphore()

    def greet(hop, carry):
        pl.semaphore_signal(
            barrier, inc=1, device_id={"hist": lax.rem(me + hop, n_hist)},
            device_id_type=pl.DeviceIdType.MESH,
        )
        return carry

    lax.fori_loop(1, n_hist, greet, 0)
    for hop in range(1, n_ka):
        pl.semaphore_signal(
            barrier, inc=1, device_id={"ka": lax.rem(my_ka + hop, n_ka)},
            device_id_type=pl.DeviceIdType.MESH,
        )

    current = step_ref[0]
    first = me * block
    before = [jnp.where(first + m < current, 1.0, 0.0) for m in range(block)]
    weight = [
        jnp.where(first + m == 0, 0.5, 1.0) * before[m] for m in range(block)
    ]

    for m in range(block):
        kw[m] = krow_ref[m].astype(jnp.float32) * weight[m]

    suffix = [None] * block
    run = jnp.zeros((orb, lanes), jnp.float32)
    for m in reversed(range(block)):
        run = run + band_ref[m] * before[m]
        suffix[m] = run
    head = run.astype(jnp.bfloat16).astype(jnp.float32)
    rest = run - head
    tail = stage.shape[1] - rows
    for d in range(per_tile):
        stage[d, rows:, :] = jnp.zeros((tail, lanes), jnp.float32)
        stage[d, rows : rows + orb, :] = head
        stage[d, rows + orb : rows + 2 * orb, :] = rest

    pl.semaphore_wait(barrier, n_hist - 1 + n_ka - 1)

    def part_copy(source, target):
        return pltpu.make_async_remote_copy(
            src_ref=psend.at[target],
            dst_ref=precv.at[source],
            send_sem=psend_sem.at[target],
            recv_sem=precv_sem.at[source],
            device_id={"hist": target},
            device_id_type=pl.DeviceIdType.MESH,
        )

    def pseudo_copy(source, target):
        return pltpu.make_async_remote_copy(
            src_ref=qsend.at[target],
            dst_ref=qrecv.at[source],
            send_sem=qsend_sem.at[target],
            recv_sem=qrecv_sem.at[source],
            device_id={"hist": target},
            device_id_type=pl.DeviceIdType.MESH,
        )

    def one_tile(tile, carry):
        at = pl.ds(pl.multiple_of(tile * tile_rows, tile_rows), tile_rows)
        zero = jnp.zeros((tile_rows, lanes), jnp.float32)
        real = [[zero] * orb for _ in range(orb)]
        imag = [[zero] * orb for _ in range(orb)]
        for m in range(block):
            for b in range(orb):
                k_re = [kw[m, 0, a, pl.ds(b, 1), :] for a in range(orb)]
                k_im = [kw[m, 1, a, pl.ds(b, 1), :] for a in range(orb)]
                for c in range(orb):
                    h_re = hist_ref[m, 0, b, c, at, :].astype(jnp.float32)
                    h_im = hist_ref[m, 1, b, c, at, :].astype(jnp.float32)
                    for a in range(orb):
                        real[a][c] += k_re[a] * h_re - k_im[a] * h_im
                        imag[a][c] += k_re[a] * h_im + k_im[a] * h_re
        for a in range(orb):
            for c in range(orb):
                out_re, out_im = zero, zero
                for b in range(orb):
                    d_re = dinv_ref[0, a, pl.ds(b, 1), :]
                    d_im = dinv_ref[1, a, pl.ds(b, 1), :]
                    out_re += d_re * real[b][c] - d_im * imag[b][c]
                    out_im += d_re * imag[b][c] + d_im * real[b][c]
                for s, value in enumerate((out_re, out_im)):
                    row = ((s * orb + a) * orb + c) * block
                    for d in range(per_tile):
                        stage[d, row : row + block, :] = value[d * block : (d + 1) * block]
        for d in range(per_tile):
            target = tile * per_tile + d
            psend[target] = stage[d].astype(jnp.bfloat16)

            @pl.when(target < me)
            def _():
                part_copy(me, target).start()

        return carry

    lax.fori_loop(0, first // tile_rows + 1, one_tile, 0)

    for s in range(2):
        for a in range(orb):
            for c in range(orb):
                row = ((s * orb + a) * orb + c) * block
                drep[row : row + block, :] = jnp.broadcast_to(
                    dinv_ref[s, a, pl.ds(c, 1), :], (block, lanes)
                )
    total[rows:, :] = jnp.ones((lanes - rows, lanes), jnp.float32)
    mult = jnp.broadcast_to(mult_ref[...].astype(jnp.float32), (8, lanes))

    eye_j = eye(times, jnp.bfloat16)
    for m in range(block):
        h_re = dot_rows(eye_j, pseudo_ref[m, 0])
        h_im = dot_rows(eye_j, pseudo_ref[m, 1])
        turned[m, 0] = jnp.concatenate([h_re, h_im], axis=1)
        turned[m, 1] = jnp.concatenate([-h_im, h_re], axis=1)

    row_of = lax.broadcasted_iota(jnp.int32, (block, 2 * states), 0)
    lane_of = lax.broadcasted_iota(jnp.int32, (block, 2 * states), 1)
    row_time = first + row_of
    row_weight = jnp.where(row_time == 0, 0.5, 1.0) * jnp.where(row_time < current, 1.0, 0.0)
    conn = jnp.concatenate([conn_ref[...], conn_ref[...]], axis=0)
    reach = lax.broadcasted_iota(jnp.int32, (2 * states, states), 1)
    eye_m = eye(block, jnp.float32)
    turned_pred = [dot_rows(eye_m, pred_ref[p], highest) for p in range(2)]
    reached = []
    for a in range(orb):
        hit = jnp.where(conn[:, 2 * a : 2 * a + 1] == reach, 1.0, 0.0) + jnp.where(
            conn[:, 2 * a + 1 : 2 * a + 2] == reach, 1.0, 0.0
        )
        reached.append(
            [dot_rows(pred, hit, highest) * row_weight * coupling for pred in turned_pred]
        )
    energies = jnp.concatenate([energy_ref[...], energy_ref[...]], axis=1)
    spins = energies * time_step * (current - row_time).astype(jnp.float32)
    free_pseudo = jnp.where(lane_of < states, -jnp.sin(spins), -jnp.cos(spins))
    free_pseudo = free_pseudo * jnp.where(row_time <= current, 1.0, 0.0)

    def take_part(source, carry):
        summed, later = carry
        part_copy(source, me).wait_recv()
        got = precv[source].astype(jnp.float32)
        summed = summed + got[:rows]
        later = later + got[rows:]
        return summed, later

    own = psend[me].astype(jnp.float32)[:rows]
    summed, later = lax.fori_loop(
        me + 1, n_hist, take_part, (own, jnp.zeros((tail, lanes), jnp.float32))
    )
    later = later[:orb] + later[orb : 2 * orb]

    for c in range(orb):
        for j in range(block):
            frep[c * block + j : c * block + j + 1, :] = (
                later[c : c + 1] + suffix[j][c : c + 1]
            )
    size = orb * block
    angle = time_step * frep[:size, :]
    when = first + lax.rem(lax.broadcasted_iota(jnp.int32, (size, lanes), 0), block)
    inside = jnp.where(when <= current, 1.0, 0.0)
    free_re = -jnp.sin(angle) * inside
    free_im = -jnp.cos(angle) * inside
    for a in range(orb):
        frep[a * size : (a + 1) * size, :] = free_re
        frep[(orb + a) * size : (orb + a + 1) * size, :] = free_im
    half = rows // 2
    f_re, f_im = frep[:half, :], frep[half:, :]
    d_re, d_im = drep[:half, :], drep[half:, :]
    total[:half, :] = summed[:half] + d_re * f_re - d_im * f_im
    total[half:rows, :] = summed[half:] + d_re * f_im + d_im * f_re

    ksend[...] = dot_rows(mult, total[...], highest)

    def local_copy(source, target):
        return pltpu.make_async_remote_copy(
            src_ref=ksend,
            dst_ref=krecv.at[source],
            send_sem=ksend_sem.at[target],
            recv_sem=krecv_sem.at[source],
            device_id={"ka": target},
            device_id_type=pl.DeviceIdType.MESH,
        )

    for hop in range(1, n_ka):
        local_copy(my_ka, lax.rem(my_ka + hop, n_ka)).start()
    lattice_out[...] = total[:rows, :].astype(jnp.bfloat16)
    local = ksend[...]
    for hop in range(1, n_ka):
        source = lax.rem(my_ka + hop, n_ka)
        local_copy(source, my_ka).wait_recv()
        local = local + krecv[source]
    local = local / local[:, rows : rows + 1]
    local_out[...] = local

    lane8 = lax.broadcasted_iota(jnp.int32, local.shape, 1)
    row8 = lax.broadcasted_iota(jnp.int32, local.shape, 0)

    def diagonal(s, a):
        lane = ((s * orb + a) * orb + a) * block + row8
        picked = jnp.where((lane8 == lane) & (row8 < block), local, 0.0)
        return jnp.sum(picked, axis=1, keepdims=True)[:block]

    self_re = jnp.zeros((block, 2 * states), jnp.float32)
    self_im = self_re
    for a in range(orb):
        h_re, h_im = diagonal(0, a), diagonal(1, a)
        r_re, r_im = reached[a]
        self_re += h_re * r_re - h_im * r_im
        self_im += h_re * r_im + h_im * r_re
    part = jnp.zeros((times, 2 * states), jnp.float32)
    for m in range(block):
        part += self_re[m : m + 1] * turned[m, 0] + self_im[m : m + 1] * turned[m, 1]
    for q in range(n_hist):
        qsend[q] = part[q * block : (q + 1) * block]

    def give_pseudo(target, carry):
        pseudo_copy(me, target).start()
        return carry

    lax.fori_loop(0, me, give_pseudo, 0)

    def take_pseudo(source, value):
        pseudo_copy(source, me).wait_recv()
        return value + qrecv[source]

    pseudo_out[...] = lax.fori_loop(me + 1, n_hist, take_pseudo, free_pseudo + qsend[me])

    def settle(target, carry):
        part_copy(me, target).wait_send()
        pseudo_copy(me, target).wait_send()
        return carry

    lax.fori_loop(0, me, settle, 0)
    for hop in range(1, n_ka):
        local_copy(my_ka, lax.rem(my_ka + hop, n_ka)).wait_send()


def per_device(
    n_hist,
    n_ka,
    step_index,
    band_energy,
    kernel_row,
    lattice_history,
    diagonal_inverse,
    multiplicity,
    state_energy,
    connection,
    predicted_row,
    pseudo_history,
):
    block, orb, lanes = band_energy.shape
    times = lattice_history.shape[4]
    states = state_energy.shape[0]
    pairs = 2 * orb * orb
    rows = pairs * block
    sent_rows = -(-(rows + 2 * orb) // tile_rows) * tile_rows
    per_tile = tile_rows // block
    vmem = pl.BlockSpec(memory_space=pltpu.VMEM)
    f32, bf16 = jnp.float32, jnp.bfloat16
    dma = pltpu.SemaphoreType.DMA
    lattice, local, pseudo = pl.pallas_call(
        functools.partial(kernel, n_hist, n_ka),
        out_shape=(
            jax.ShapeDtypeStruct((rows, lanes), bf16),
            jax.ShapeDtypeStruct((8, lanes), f32),
            jax.ShapeDtypeStruct((block, 2 * states), f32),
        ),
        in_specs=[pl.BlockSpec(memory_space=pltpu.SMEM)] + [vmem] * 9,
        out_specs=(vmem, vmem, vmem),
        scratch_shapes=[
            pltpu.VMEM(kernel_row.shape, f32),
            pltpu.VMEM((per_tile, sent_rows, lanes), f32),
            pltpu.VMEM((n_hist, sent_rows, lanes), bf16),
            pltpu.VMEM((n_hist, sent_rows, lanes), bf16),
            pltpu.VMEM((rows, lanes), f32),
            pltpu.VMEM((rows, lanes), f32),
            pltpu.VMEM((lanes, lanes), f32),
            pltpu.VMEM((8, lanes), f32),
            pltpu.VMEM((n_ka, 8, lanes), f32),
            pltpu.VMEM((block, 2, times, 2 * states), f32),
            pltpu.VMEM((n_hist, block, 2 * states), f32),
            pltpu.VMEM((n_hist, block, 2 * states), f32),
            dma((n_hist,)),
            dma((n_hist,)),
            dma((n_ka,)),
            dma((n_ka,)),
            dma((n_hist,)),
            dma((n_hist,)),
        ],
        compiler_params=pltpu.CompilerParams(collective_id=0, has_side_effects=True),
    )(
        step_index,
        band_energy,
        kernel_row,
        lattice_history,
        diagonal_inverse,
        multiplicity[None],
        state_energy[None],
        connection,
        predicted_row,
        pseudo_history,
    )
    lattice_row = jnp.transpose(lattice.reshape(pairs, block, lanes), (1, 0, 2)).reshape(
        block, 2, orb, orb, lanes
    )
    local_row = local[0, :rows].reshape(2, orb, orb, block)
    pseudo_row = jnp.transpose(pseudo.reshape(block, 2, states), (1, 2, 0))
    return lattice_row, local_row, pseudo_row


def solution(mesh):
    in_specs = (
        P(),
        P("hist", None, "ka"),
        P("hist", None, None, None, "ka"),
        P("hist", None, None, None, None, "ka"),
        P(None, None, None, "ka"),
        P("ka"),
        P(),
        P(),
        P(None, None, "hist"),
        P("hist", None, None, None),
    )
    out_specs = (
        P("hist", None, None, None, "ka"),
        P(None, None, None, "hist"),
        P(None, None, "hist"),
    )
    return jax.shard_map(
        functools.partial(per_device, mesh.shape["hist"], mesh.shape["ka"]),
        mesh=mesh,
        in_specs=in_specs,
        out_specs=out_specs,
        check_vma=False,
    )
```

time: 131 us -> 28.7 us (0.22)
  blocking collectives: 87.1 us -> 0 us
  Pallas kernels: 0 us -> 18.9 us
  matrix products: 18.5 us -> 0 us
  starting transfers between devices: 6.49 us -> 0 us
  other arithmetic: 3.97 us -> 0 us
  local copies, waits for them, and re-layouts: 11.9 us -> 8.17 us
    all_gather x2 -> x0, blocking collectives: 35 us -> none  [the longest x1 22.2 us: per_device(): full_kernel = lax.all_gather(kernel, 'hist', axis=0, tiled=True)]
    psum x2 -> x0, blocking collectives: 26.2 us -> none  [the longest x1 15.3 us: per_device(): upto_now = lax.psum(masked_sum, 'hist')]
    unnamed x1 -> x0, blocking collectives: 25.9 us -> none
    pallas_call x0 -> x1, Pallas kernels: none -> 18.9 us  [per_device(): pl.pallas_call(functools.partial(kernel, n_hist, n_ka), out_shape=(jax.Sh...]
    dot_general x7 -> x0, matrix products: 18.5 us -> none  [the longest x1 10.3 us: per_device(): jnp.einsum('msapbk,mpbcjk->jsack', complex_form(full_kernel), columns, pr...]
    all_to_all x1 -> x0, starting transfers between devices: 6.49 us -> none  [per_device(): lax.all_to_all(lattice_history, 'hist', split_axis=4, concat_axis=0, tile...]
    all_to_all x2 -> x0, local copies, waits for them, and re-layouts: 3.59 us -> none  [per_device(): lax.all_to_all(lattice_history, 'hist', split_axis=4, concat_axis=0, tile...]
    another operation x3 -> x1, local copies, waits for them, and re-layouts: 3.02 us -> 0.09 us  [per_device(): local_row = local[0, :rows].reshape(2, orb, orb, block)]
  transfers between devices with their start and end apart: 1 -> 0, of which waited for: 0 -> 0; matrix products, arithmetic and copies ran while one was open for 4% -> 0% of each run, Pallas kernels for 0% -> 0%
where the time goes in v1:
time: 28.7 us; the launch traced here: 28.4 us
  Pallas kernels  18.9 us (66%)
  local copies, waits for them, and re-layouts  8.17 us (28%)
  between operations  1.32 us (5%)
    pallas_call x1, Pallas kernels, per_device(): pl.pallas_call(functools.partial(kernel, n_hist, n_ka), out_shape=(jax.Sh...  18.9 us
    unnamed x20, local copies, waits for them, and re-layouts  6.71 us
    slice x1, local copies, waits for them, and re-layouts, per_device(): local_row = local[0, :rows].reshape(2, orb, orb, block)  0.7 us
    reshape x2, local copies, waits for them, and re-layouts, per_device(): pseudo_row = jnp.transpose(pseudo.reshape(block, 2, states), (1, 2, 0))  0.68 us

profile of v1, /device:TPU:0, one launch (start us, length us, event | category | flops | bytes accessed | tf_op | source)
XLA Modules:
  0.0 28.4 jit_solution(7903316066520789368)
XLA Ops:
  1.3 0.0 copy-start.2
  1.3 0.0 copy-start.1
  1.3 1.3 %copy.21.band_ref = f32[4,3,128]{2,1,0:T(4,128)} copy(f32[4,3,128]{2,0,1:T(4,128)} %param.11) | data formatting | bytes 12288 | tf_op args[1]
  2.6 0.0 copy-done.2
  2.6 0.6 %copy.23.dinv_ref = f32[2,3,3,128]{3,2,1,0:T(4,128)} copy(f32[2,3,3,128]{3,0,2,1:T(2,128)S(1)} %copy-done.2) | data formatting | bytes 18432 | tf_op args[4]
  3.2 0.0 copy-done.1
  3.2 0.0 copy-start
  3.2 0.6 %copy.22.krow_ref = bf16[4,2,3,3,128]{4,3,2,1,0:T(4,128)(2,1)} copy(bf16[4,2,3,3,128]{4,1,3,2,0:T(2,128)(2,1)S(1)} %copy-done.1) | data formatting | bytes 36864 | tf_op args[2]
  3.8 0.0 copy-done.3
  3.8 0.0 copy-start.4
  3.8 0.7 %copy.24.conn_ref = s32[64,6]{1,0:T(8,128)} copy(s32[64,6]{0,1:T(8,128)S(1)} %copy-done.3) | data formatting | bytes 3072 | tf_op args[7]
  4.5 0.0 copy-done.4
  4.5 0.7 %copy.25.pred_ref = f32[2,64,4]{2,1,0:T(8,128)} copy(f32[2,64,4]{1,2,0:T(4,128)S(1)} %copy-done.4) | data formatting | bytes 4096 | tf_op args[8]
  5.3 0.0 copy-done
  5.3 0.8 %copy.26.pseudo_ref = bf16[4,2,64,32]{3,2,1,0:T(8,128)(2,1)} copy(bf16[4,2,64,32]{2,3,1,0:T(8,128)(2,1)S(1)} %copy-done) | data formatting | bytes 65536 | tf_op args[9]
  6.0 18.9 %shard_map.121 = (bf16[72,128]{1,0:T(8,128)(2,1)}, f32[8,128]{1,0:T(8,128)}, f32[4,128]{1,0:T(4,128)}) custom-call(s32[1]{0:T(128)S(6)} %copy.32.step_ref, f32[4,3,128]{2,1,0:T(4,128)} %copy.21.band_ref, bf16[4,2,3,3,128]{4,3,2,1,0:T(4,128)(2,1)} %copy.22.krow_ref, bf16[4,2,3,3,32,128]{5,4,3,2,1,0:T(8,128)(2,1)} %hist_ref.1, ...), custom_call_target="tpu_custom_call" | custom-call | tf_op jit(solution)/shard_map/pallas_call | solution.py:338
  25.0 0.0 copy-start.5
  25.0 1.3 %copy.28 = bf16[4,2,3,3,128]{4,1,3,2,0:T(2,128)(2,1)} copy(bf16[4,2,3,3,128]{4,0,3,2,1:T(4,128)(2,1)} %bitcast.10) | data formatting | bytes 36864
  26.3 0.7 %slice_reduce_fusion = f32[72]{0:T(128)S(1)} fusion(f32[8,128]{1,0:T(8,128)} %get-tuple-element.7), kind=kLoop, calls=%fused_computation.1 | loop fusion | bytes 576 | tf_op jit(solution)/shard_map/slice | solution.py:383
  27.0 0.0 copy-done.5
  27.0 0.1 reshape.17
  27.1 0.6 %copy.31 = f32[4,2,64]{2,0,1:T(4,128)} copy(f32[4,2,64]{2,1,0:T(2,128)S(1)} %reshape.17) | data formatting | bytes 4096 | tf_op jit(solution)/shard_map/reshape | solution.py:384
  27.7 0.1 reshape_squeeze.3
  27.8 0.6 %copy.29 = f32[2,3,3,4]{3,0,2,1:T(2,128)} copy(f32[2,3,3,4]{3,2,1,0:T(4,128)S(1)} %reshape_squeeze.3) | data formatting | bytes 576
  (1 shorter events, 0.0 us)
Async XLA Ops:
  1.3 1.3 %copy-start.2 = (f32[2,3,3,128]{3,0,2,1:T(2,128)S(1)}, f32[2,3,3,128]{3,0,2,1:T(2,128)}, u32[]{:S(2)}) copy-start(f32[2,3,3,128]{3,0,2,1:T(2,128)} %param.14) | copy-start | bytes 27652
  1.3 1.9 %copy-start.1 = (bf16[4,2,3,3,128]{4,1,3,2,0:T(2,128)(2,1)S(1)}, bf16[4,2,3,3,128]{4,1,3,2,0:T(2,128)(2,1)}, u32[]{:S(2)}) copy-start(bf16[4,2,3,3,128]{4,1,3,2,0:T(2,128)(2,1)} %param.12) | copy-start | bytes 55300
  2.6 1.2 %copy-start.3 = (s32[64,6]{0,1:T(8,128)S(1)}, s32[64,6]{0,1:T(8,128)}, u32[]{:S(2)}) copy-start(s32[64,6]{0,1:T(8,128)} %param.17) | copy-start | bytes 4612
  3.2 2.1 %copy-start = (bf16[4,2,64,32]{2,3,1,0:T(8,128)(2,1)S(1)}, bf16[4,2,64,32]{2,3,1,0:T(8,128)(2,1)}, u32[]{:S(2)}) copy-start(bf16[4,2,64,32]{2,3,1,0:T(8,128)(2,1)} %param.19) | copy-start | bytes 98308
  3.8 0.7 %copy-start.4 = (f32[2,64,4]{1,2,0:T(4,128)S(1)}, f32[2,64,4]{1,2,0:T(4,128)}, u32[]{:S(2)}) copy-start(f32[2,64,4]{1,2,0:T(4,128)} %param.18) | copy-start | bytes 6148
  25.0 2.1 %copy-start.5 = (f32[4,128]{1,0:T(4,128)S(1)}, f32[4,128]{1,0:T(4,128)}, u32[]{:S(2)}) copy-start(f32[4,128]{1,0:T(4,128)} %get-tuple-element.8) | copy-start | bytes 6148

commit v2 on v1

--- a/solution.py
+++ b/solution.py
@@ -21,12 +21,6 @@
         precision=precision,
         preferred_element_type=jnp.float32,
     )
-
-
-def eye(size, dtype):
-    rows = lax.broadcasted_iota(jnp.int32, (size, size), 0)
-    cols = lax.broadcasted_iota(jnp.int32, (size, size), 1)
-    return jnp.where(rows == cols, 1.0, 0.0).astype(dtype)
 
 
 def kernel(
@@ -46,6 +40,7 @@
     local_out,
     pseudo_out,
     kw,
+    suffix,
     stage,
     psend,
     precv,
@@ -64,7 +59,7 @@
     qsend_sem,
     qrecv_sem,
 ):
-    block, orb, lanes = band_ref.shape
+    orb, block, lanes = band_ref.shape
     times = hist_ref.shape[4]
     states = energy_ref.shape[1]
     pairs = 2 * orb * orb
@@ -99,18 +94,19 @@
     for m in range(block):
         kw[m] = krow_ref[m].astype(jnp.float32) * weight[m]
 
-    suffix = [None] * block
-    run = jnp.zeros((orb, lanes), jnp.float32)
-    for m in reversed(range(block)):
-        run = run + band_ref[m] * before[m]
-        suffix[m] = run
-    head = run.astype(jnp.bfloat16).astype(jnp.float32)
-    rest = run - head
     tail = stage.shape[1] - rows
     for d in range(per_tile):
         stage[d, rows:, :] = jnp.zeros((tail, lanes), jnp.float32)
-        stage[d, rows : rows + orb, :] = head
-        stage[d, rows + orb : rows + 2 * orb, :] = rest
+    for c in range(orb):
+        run = jnp.zeros((1, lanes), jnp.float32)
+        for m in reversed(range(block)):
+            run = run + band_ref[c, m : m + 1, :] * before[m]
+            suffix[c * block + m : c * block + m + 1, :] = run
+        head = run.astype(jnp.bfloat16).astype(jnp.float32)
+        rest = run - head
+        for d in range(per_tile):
+            stage[d, rows + c : rows + c + 1, :] = head
+            stage[d, rows + orb + c : rows + orb + c + 1, :] = rest
 
     pl.semaphore_wait(barrier, n_hist - 1 + n_ka - 1)
 
@@ -141,8 +137,8 @@
         imag = [[zero] * orb for _ in range(orb)]
         for m in range(block):
             for b in range(orb):
-                k_re = [kw[m, 0, a, pl.ds(b, 1), :] for a in range(orb)]
-                k_im = [kw[m, 1, a, pl.ds(b, 1), :] for a in range(orb)]
+                k_re = [kw[m, a, b, 0:1, :] for a in range(orb)]
+                k_im = [kw[m, a, b, 1:2, :] for a in range(orb)]
                 for c in range(orb):
                     h_re = hist_ref[m, 0, b, c, at, :].astype(jnp.float32)
                     h_im = hist_ref[m, 1, b, c, at, :].astype(jnp.float32)
@@ -153,8 +149,8 @@
             for c in range(orb):
                 out_re, out_im = zero, zero
                 for b in range(orb):
-                    d_re = dinv_ref[0, a, pl.ds(b, 1), :]
-                    d_im = dinv_ref[1, a, pl.ds(b, 1), :]
+                    d_re = dinv_ref[a, b, 0:1, :]
+                    d_im = dinv_ref[a, b, 1:2, :]
                     out_re += d_re * real[b][c] - d_im * imag[b][c]
                     out_im += d_re * imag[b][c] + d_im * real[b][c]
                 for s, value in enumerate((out_re, out_im)):
@@ -178,15 +174,14 @@
             for c in range(orb):
                 row = ((s * orb + a) * orb + c) * block
                 drep[row : row + block, :] = jnp.broadcast_to(
-                    dinv_ref[s, a, pl.ds(c, 1), :], (block, lanes)
+                    dinv_ref[a, c, s : s + 1, :], (block, lanes)
                 )
     total[rows:, :] = jnp.ones((lanes - rows, lanes), jnp.float32)
     mult = jnp.broadcast_to(mult_ref[...].astype(jnp.float32), (8, lanes))
 
-    eye_j = eye(times, jnp.bfloat16)
     for m in range(block):
-        h_re = dot_rows(eye_j, pseudo_ref[m, 0])
-        h_im = dot_rows(eye_j, pseudo_ref[m, 1])
+        h_re = pseudo_ref[m, 0].astype(jnp.float32)
+        h_im = pseudo_ref[m, 1].astype(jnp.float32)
         turned[m, 0] = jnp.concatenate([h_re, h_im], axis=1)
         turned[m, 1] = jnp.concatenate([-h_im, h_re], axis=1)
 
@@ -194,17 +189,20 @@
     lane_of = lax.broadcasted_iota(jnp.int32, (block, 2 * states), 1)
     row_time = first + row_of
     row_weight = jnp.where(row_time == 0, 0.5, 1.0) * jnp.where(row_time < current, 1.0, 0.0)
-    conn = jnp.concatenate([conn_ref[...], conn_ref[...]], axis=0)
-    reach = lax.broadcasted_iota(jnp.int32, (2 * states, states), 1)
-    eye_m = eye(block, jnp.float32)
-    turned_pred = [dot_rows(eye_m, pred_ref[p], highest) for p in range(2)]
+    conn = jnp.concatenate([conn_ref[...], conn_ref[...]], axis=1)
+    reach = lax.broadcasted_iota(jnp.int32, (states, 2 * states), 0)
     reached = []
     for a in range(orb):
-        hit = jnp.where(conn[:, 2 * a : 2 * a + 1] == reach, 1.0, 0.0) + jnp.where(
-            conn[:, 2 * a + 1 : 2 * a + 2] == reach, 1.0, 0.0
+        hit = jnp.where(conn[2 * a : 2 * a + 1] == reach, 1.0, 0.0) + jnp.where(
+            conn[2 * a + 1 : 2 * a + 2] == reach, 1.0, 0.0
         )
         reached.append(
-            [dot_rows(pred, hit, highest) * row_weight * coupling for pred in turned_pred]
+            [
+                jnp.dot(pred_ref[p], hit, precision=highest, preferred_element_type=jnp.float32)
+                * row_weight
+                * coupling
+                for p in range(2)
+            ]
         )
     energies = jnp.concatenate([energy_ref[...], energy_ref[...]], axis=1)
     spins = energies * time_step * (current - row_time).astype(jnp.float32)
@@ -228,7 +226,7 @@
     for c in range(orb):
         for j in range(block):
             frep[c * block + j : c * block + j + 1, :] = (
-                later[c : c + 1] + suffix[j][c : c + 1]
+                later[c : c + 1] + suffix[c * block + j : c * block + j + 1, :]
             )
     size = orb * block
     angle = time_step * frep[:size, :]
@@ -259,14 +257,17 @@
 
     for hop in range(1, n_ka):
         local_copy(my_ka, lax.rem(my_ka + hop, n_ka)).start()
-    lattice_out[...] = total[:rows, :].astype(jnp.bfloat16)
+    for a in range(orb):
+        for c in range(orb):
+            for j in range(block):
+                pair = total[pl.ds((a * orb + c) * block + j, 2, stride=half), :]
+                lattice_out[j, a, c] = pair.astype(jnp.bfloat16)
     local = ksend[...]
     for hop in range(1, n_ka):
         source = lax.rem(my_ka + hop, n_ka)
         local_copy(source, my_ka).wait_recv()
         local = local + krecv[source]
     local = local / local[:, rows : rows + 1]
-    local_out[...] = local
 
     lane8 = lax.broadcasted_iota(jnp.int32, local.shape, 1)
     row8 = lax.broadcasted_iota(jnp.int32, local.shape, 0)
@@ -295,11 +296,19 @@
 
     lax.fori_loop(0, me, give_pseudo, 0)
 
+    for s in range(2):
+        for a in range(orb):
+            for c in range(orb):
+                row = ((s * orb + a) * orb + c) * block
+                local_out[a, c, s : s + 1, :] = local[0:1, row : row + block]
+
     def take_pseudo(source, value):
         pseudo_copy(source, me).wait_recv()
         return value + qrecv[source]
 
-    pseudo_out[...] = lax.fori_loop(me + 1, n_hist, take_pseudo, free_pseudo + qsend[me])
+    value = lax.fori_loop(me + 1, n_hist, take_pseudo, free_pseudo + qsend[me])
+    for p in range(2):
+        pseudo_out[p] = value[:, p * states : (p + 1) * states]
 
     def settle(target, carry):
         part_copy(me, target).wait_send()
@@ -338,14 +347,15 @@
     lattice, local, pseudo = pl.pallas_call(
         functools.partial(kernel, n_hist, n_ka),
         out_shape=(
-            jax.ShapeDtypeStruct((rows, lanes), bf16),
-            jax.ShapeDtypeStruct((8, lanes), f32),
-            jax.ShapeDtypeStruct((block, 2 * states), f32),
+            jax.ShapeDtypeStruct((block, orb, orb, 2, lanes), bf16),
+            jax.ShapeDtypeStruct((orb, orb, 2, block), f32),
+            jax.ShapeDtypeStruct((2, block, states), f32),
         ),
         in_specs=[pl.BlockSpec(memory_space=pltpu.SMEM)] + [vmem] * 9,
         out_specs=(vmem, vmem, vmem),
         scratch_shapes=[
-            pltpu.VMEM(kernel_row.shape, f32),
+            pltpu.VMEM((block, orb, orb, 2, lanes), f32),
+            pltpu.VMEM((orb * block, lanes), f32),
             pltpu.VMEM((per_tile, sent_rows, lanes), f32),
             pltpu.VMEM((n_hist, sent_rows, lanes), bf16),
             pltpu.VMEM((n_hist, sent_rows, lanes), bf16),
@@ -367,22 +377,21 @@
         compiler_params=pltpu.CompilerParams(collective_id=0, has_side_effects=True),
     )(
         step_index,
-        band_energy,
-        kernel_row,
+        jnp.transpose(band_energy, (1, 0, 2)),
+        jnp.transpose(kernel_row, (0, 2, 3, 1, 4)),
         lattice_history,
-        diagonal_inverse,
+        jnp.transpose(diagonal_inverse, (1, 2, 0, 3)),
         multiplicity[None],
         state_energy[None],
-        connection,
-        predicted_row,
-        pseudo_history,
-    )
-    lattice_row = jnp.transpose(lattice.reshape(pairs, block, lanes), (1, 0, 2)).reshape(
-        block, 2, orb, orb, lanes
-    )
-    local_row = local[0, :rows].reshape(2, orb, orb, block)
-    pseudo_row = jnp.transpose(pseudo.reshape(block, 2, states), (1, 2, 0))
-    return lattice_row, local_row, pseudo_row
+        jnp.transpose(connection),
+        jnp.transpose(predicted_row, (0, 2, 1)),
+        jnp.transpose(pseudo_history, (0, 1, 3, 2)),
+    )
+    return (
+        jnp.transpose(lattice, (0, 3, 1, 2, 4)),
+        jnp.transpose(local, (2, 0, 1, 3)),
+        jnp.transpose(pseudo, (0, 2, 1)),
+    )
 
 
 def solution(mesh):

time: 28.7 us -> 23 us (0.80)
  local copies, waits for them, and re-layouts: 8.17 us -> 2.63 us
    unnamed x20 -> x7, local copies, waits for them, and re-layouts: 6.71 us -> 2.63 us
    slice x1 -> x0, local copies, waits for them, and re-layouts: 0.7 us -> none  [per_device(): local_row = local[0, :rows].reshape(2, orb, orb, block)]
    reshape x2 -> x0, local copies, waits for them, and re-layouts: 0.68 us -> none  [per_device(): pseudo_row = jnp.transpose(pseudo.reshape(block, 2, states), (1, 2, 0))]
where the time goes in v2:
time: 23 us; the launch traced here: 22.7 us
  Pallas kernels  18.8 us (82%)
  local copies, waits for them, and re-layouts  2.63 us (11%)
  between operations  1.3 us (6%)
    pallas_call x1, Pallas kernels, per_device(): pl.pallas_call(functools.partial(kernel, n_hist, n_ka), out_shape=(jax.Sh...  18.8 us
    unnamed x7, local copies, waits for them, and re-layouts  2.63 us

profile of v2, /device:TPU:0, one launch (start us, length us, event | category | flops | bytes accessed | tf_op | source)
XLA Modules:
  0.0 22.7 jit_solution(18321847466407232613)
XLA Ops:
  1.3 18.8 %shard_map.121 = (bf16[4,3,3,2,128]{4,3,2,1,0:T(2,128)(2,1)}, f32[3,3,2,4]{3,2,1,0:T(2,128)}, f32[2,4,64]{2,1,0:T(4,128)}) custom-call(s32[1]{0:T(128)S(6)} %copy.16.step_ref, f32[3,4,128]{2,1,0:T(4,128)} %bitcast.16, bf16[4,3,3,2,128]{4,3,2,1,0:T(2,128)(2,1)} %bitcast.12, bf16[4,2,3,3,32,128]{5,4,3,2,1,0:T(8,128)(2,1)} %hist_ref.1, ...), custom_call_target="tpu_custom_call" | custom-call | tf_op jit(solution)/shard_map/pallas_call | solution.py:347
  20.1 0.0 copy-start
  20.1 1.3 %copy.17 = bf16[4,2,3,3,128]{4,1,3,2,0:T(2,128)(2,1)} copy(bf16[4,2,3,3,128]{4,1,3,2,0:T(2,128)(2,1)} %bitcast.13) | data formatting | bytes 36864
  21.5 0.0 copy-done
  21.5 0.0 copy-start.1
  21.5 0.6 %copy.18 = f32[2,3,3,4]{3,0,2,1:T(2,128)} copy(f32[2,3,3,4]{3,0,2,1:T(2,128)S(1)} %bitcast.14) | data formatting | bytes 576
  22.1 0.1 copy-done.1
  22.1 0.6 %copy.19 = f32[2,64,4]{1,2,0:T(4,128)} copy(f32[2,64,4]{1,2,0:T(4,128)S(1)} %bitcast.19) | data formatting | bytes 4096
Async XLA Ops:
  20.1 1.4 %copy-start = (f32[3,3,2,4]{3,2,1,0:T(2,128)S(1)}, f32[3,3,2,4]{3,2,1,0:T(2,128)}, u32[]{:S(2)}) copy-start(f32[3,3,2,4]{3,2,1,0:T(2,128)} %get-tuple-element.7) | copy-start | bytes 868
  21.5 0.7 %copy-start.1 = (f32[2,4,64]{2,1,0:T(4,128)S(1)}, f32[2,4,64]{2,1,0:T(4,128)}, u32[]{:S(2)}) copy-start(f32[2,4,64]{2,1,0:T(4,128)} %get-tuple-element.8) | copy-start | bytes 6148

commit v3 on v2

--- a/solution.py
+++ b/solution.py
@@ -36,12 +36,17 @@
     conn_ref,
     pred_ref,
     pseudo_ref,
-    lattice_out,
+    total_out,
     local_out,
     pseudo_out,
+    hist_vmem,
     kw,
     suffix,
     stage,
+    esend,
+    erecv,
+    lsend,
+    lrecv,
     psend,
     precv,
     drep,
@@ -52,6 +57,11 @@
     turned,
     qsend,
     qrecv,
+    hist_sem,
+    esend_sem,
+    erecv_sem,
+    lsend_sem,
+    lrecv_sem,
     psend_sem,
     precv_sem,
     ksend_sem,
@@ -68,6 +78,8 @@
     me = lax.axis_index("hist")
     my_ka = lax.axis_index("ka")
 
+    load = pltpu.make_async_copy(hist_ref, hist_vmem, hist_sem)
+    load.start()
     barrier = pltpu.get_barrier_semaphore()
 
     def greet(hop, carry):
@@ -94,41 +106,45 @@
     for m in range(block):
         kw[m] = krow_ref[m].astype(jnp.float32) * weight[m]
 
-    tail = stage.shape[1] - rows
-    for d in range(per_tile):
-        stage[d, rows:, :] = jnp.zeros((tail, lanes), jnp.float32)
+    esend[...] = jnp.zeros(esend.shape, jnp.float32)
     for c in range(orb):
         run = jnp.zeros((1, lanes), jnp.float32)
         for m in reversed(range(block)):
             run = run + band_ref[c, m : m + 1, :] * before[m]
             suffix[c * block + m : c * block + m + 1, :] = run
-        head = run.astype(jnp.bfloat16).astype(jnp.float32)
-        rest = run - head
-        for d in range(per_tile):
-            stage[d, rows + c : rows + c + 1, :] = head
-            stage[d, rows + orb + c : rows + orb + c + 1, :] = rest
+        esend[c : c + 1, :] = run
+    mult = jnp.broadcast_to(mult_ref[...].astype(jnp.float32), (8, lanes))
 
     pl.semaphore_wait(barrier, n_hist - 1 + n_ka - 1)
 
-    def part_copy(source, target):
+    def hist_copy(src, dst, send_sem, recv_sem, source, target):
         return pltpu.make_async_remote_copy(
-            src_ref=psend.at[target],
-            dst_ref=precv.at[source],
-            send_sem=psend_sem.at[target],
-            recv_sem=precv_sem.at[source],
+            src_ref=src,
+            dst_ref=dst.at[source],
+            send_sem=send_sem.at[target],
+            recv_sem=recv_sem.at[source],
             device_id={"hist": target},
             device_id_type=pl.DeviceIdType.MESH,
         )
 
+    def energy_copy(source, target):
+        return hist_copy(esend, erecv, esend_sem, erecv_sem, source, target)
+
+    def sum_copy(source, target):
+        return hist_copy(lsend.at[target], lrecv, lsend_sem, lrecv_sem, source, target)
+
+    def part_copy(source, target):
+        return hist_copy(psend.at[target], precv, psend_sem, precv_sem, source, target)
+
     def pseudo_copy(source, target):
-        return pltpu.make_async_remote_copy(
-            src_ref=qsend.at[target],
-            dst_ref=qrecv.at[source],
-            send_sem=qsend_sem.at[target],
-            recv_sem=qrecv_sem.at[source],
-            device_id={"hist": target},
-            device_id_type=pl.DeviceIdType.MESH,
-        )
+        return hist_copy(qsend.at[target], qrecv, qsend_sem, qrecv_sem, source, target)
+
+    def give_energy(target, carry):
+        energy_copy(me, target).start()
+        return carry
+
+    lax.fori_loop(0, me, give_energy, 0)
+    load.wait()
 
     def one_tile(tile, carry):
         at = pl.ds(pl.multiple_of(tile * tile_rows, tile_rows), tile_rows)
@@ -140,8 +156,8 @@
                 k_re = [kw[m, a, b, 0:1, :] for a in range(orb)]
                 k_im = [kw[m, a, b, 1:2, :] for a in range(orb)]
                 for c in range(orb):
-                    h_re = hist_ref[m, 0, b, c, at, :].astype(jnp.float32)
-                    h_im = hist_ref[m, 1, b, c, at, :].astype(jnp.float32)
+                    h_re = hist_vmem[m, 0, b, c, at, :].astype(jnp.float32)
+                    h_im = hist_vmem[m, 1, b, c, at, :].astype(jnp.float32)
                     for a in range(orb):
                         real[a][c] += k_re[a] * h_re - k_im[a] * h_im
                         imag[a][c] += k_re[a] * h_im + k_im[a] * h_re
@@ -159,15 +175,23 @@
                         stage[d, row : row + block, :] = value[d * block : (d + 1) * block]
         for d in range(per_tile):
             target = tile * per_tile + d
-            psend[target] = stage[d].astype(jnp.bfloat16)
+            lsend[target, :, :rows] = dot_rows(mult, stage[d], highest)[:1]
 
             @pl.when(target < me)
             def _():
-                part_copy(me, target).start()
-
+                sum_copy(me, target).start()
+
+        for d in range(per_tile):
+            psend[tile * per_tile + d] = stage[d].astype(jnp.bfloat16)
         return carry
 
     lax.fori_loop(0, first // tile_rows + 1, one_tile, 0)
+
+    def give_part(target, carry):
+        part_copy(me, target).start()
+        return carry
+
+    lax.fori_loop(0, me, give_part, 0)
 
     for s in range(2):
         for a in range(orb):
@@ -177,8 +201,6 @@
                     dinv_ref[a, c, s : s + 1, :], (block, lanes)
                 )
     total[rows:, :] = jnp.ones((lanes - rows, lanes), jnp.float32)
-    mult = jnp.broadcast_to(mult_ref[...].astype(jnp.float32), (8, lanes))
-
     for m in range(block):
         h_re = pseudo_ref[m, 0].astype(jnp.float32)
         h_im = pseudo_ref[m, 1].astype(jnp.float32)
@@ -209,20 +231,13 @@
     free_pseudo = jnp.where(lane_of < states, -jnp.sin(spins), -jnp.cos(spins))
     free_pseudo = free_pseudo * jnp.where(row_time <= current, 1.0, 0.0)
 
-    def take_part(source, carry):
-        summed, later = carry
-        part_copy(source, me).wait_recv()
-        got = precv[source].astype(jnp.float32)
-        summed = summed + got[:rows]
-        later = later + got[rows:]
-        return summed, later
-
-    own = psend[me].astype(jnp.float32)[:rows]
-    summed, later = lax.fori_loop(
-        me + 1, n_hist, take_part, (own, jnp.zeros((tail, lanes), jnp.float32))
-    )
-    later = later[:orb] + later[orb : 2 * orb]
-
+    def take_energy(source, later):
+        energy_copy(source, me).wait_recv()
+        return later + erecv[source]
+
+    later = lax.fori_loop(
+        me + 1, n_hist, take_energy, jnp.zeros(esend.shape, jnp.float32)
+    )
     for c in range(orb):
         for j in range(block):
             frep[c * block + j : c * block + j + 1, :] = (
@@ -240,10 +255,18 @@
     half = rows // 2
     f_re, f_im = frep[:half, :], frep[half:, :]
     d_re, d_im = drep[:half, :], drep[half:, :]
-    total[:half, :] = summed[:half] + d_re * f_re - d_im * f_im
-    total[half:rows, :] = summed[half:] + d_re * f_im + d_im * f_re
-
-    ksend[...] = dot_rows(mult, total[...], highest)
+    total[:half, :] = d_re * f_re - d_im * f_im
+    total[half:rows, :] = d_re * f_im + d_im * f_re
+
+    free_sums = dot_rows(mult, total[...], highest)[:1]
+
+    def take_sum(source, value):
+        sum_copy(source, me).wait_recv()
+        return value + lrecv[source][:, :rows]
+
+    own_sums = lsend[me][:, :rows] + free_sums[:, :rows]
+    ksend[...] = free_sums
+    ksend[:, :rows] = lax.fori_loop(me + 1, n_hist, take_sum, own_sums)
 
     def local_copy(source, target):
         return pltpu.make_async_remote_copy(
@@ -257,17 +280,13 @@
 
     for hop in range(1, n_ka):
         local_copy(my_ka, lax.rem(my_ka + hop, n_ka)).start()
-    for a in range(orb):
-        for c in range(orb):
-            for j in range(block):
-                pair = total[pl.ds((a * orb + c) * block + j, 2, stride=half), :]
-                lattice_out[j, a, c] = pair.astype(jnp.bfloat16)
     local = ksend[...]
     for hop in range(1, n_ka):
         source = lax.rem(my_ka + hop, n_ka)
         local_copy(source, my_ka).wait_recv()
         local = local + krecv[source]
-    local = local / local[:, rows : rows + 1]
+    local = jnp.broadcast_to(local / local[:, rows : rows + 1], (8, lanes))
+    local_out[...] = local
 
     lane8 = lax.broadcasted_iota(jnp.int32, local.shape, 1)
     row8 = lax.broadcasted_iota(jnp.int32, local.shape, 0)
@@ -296,21 +315,22 @@
 
     lax.fori_loop(0, me, give_pseudo, 0)
 
-    for s in range(2):
-        for a in range(orb):
-            for c in range(orb):
-                row = ((s * orb + a) * orb + c) * block
-                local_out[a, c, s : s + 1, :] = local[0:1, row : row + block]
+    def take_part(source, value):
+        part_copy(source, me).wait_recv()
+        return value + precv[source].astype(jnp.float32)
+
+    fresh = total[:rows, :] + psend[me].astype(jnp.float32)
+    total_out[...] = lax.fori_loop(me + 1, n_hist, take_part, fresh)
 
     def take_pseudo(source, value):
         pseudo_copy(source, me).wait_recv()
         return value + qrecv[source]
 
-    value = lax.fori_loop(me + 1, n_hist, take_pseudo, free_pseudo + qsend[me])
-    for p in range(2):
-        pseudo_out[p] = value[:, p * states : (p + 1) * states]
+    pseudo_out[...] = lax.fori_loop(me + 1, n_hist, take_pseudo, free_pseudo + qsend[me])
 
     def settle(target, carry):
+        energy_copy(me, target).wait_send()
+        sum_copy(me, target).wait_send()
         part_copy(me, target).wait_send()
         pseudo_copy(me, target).wait_send()
         return carry
@@ -318,6 +338,23 @@
     lax.fori_loop(0, me, settle, 0)
     for hop in range(1, n_ka):
         local_copy(my_ka, lax.rem(my_ka + hop, n_ka)).wait_send()
+
+
+def lay_out(total_ref, local_ref, pseudo_ref, lattice_out, local_out, pseudo_out):
+    block, orb = lattice_out.shape[:2]
+    states = pseudo_out.shape[2]
+    half = total_ref.shape[0] // 2
+    for a in range(orb):
+        for c in range(orb):
+            row = (a * orb + c) * block
+            for j in range(block):
+                pair = total_ref[pl.ds(row + j, 2, stride=half), :]
+                lattice_out[j, a, c] = pair.astype(jnp.bfloat16)
+            for s in range(2):
+                at = s * half + row
+                local_out[a, c, s : s + 1, :] = local_ref[0:1, at : at + block]
+    for p in range(2):
+        pseudo_out[p] = pseudo_ref[:, p * states : (p + 1) * states]
 
 
 def per_device(
@@ -339,34 +376,44 @@
     states = state_energy.shape[0]
     pairs = 2 * orb * orb
     rows = pairs * block
-    sent_rows = -(-(rows + 2 * orb) // tile_rows) * tile_rows
     per_tile = tile_rows // block
     vmem = pl.BlockSpec(memory_space=pltpu.VMEM)
     f32, bf16 = jnp.float32, jnp.bfloat16
     dma = pltpu.SemaphoreType.DMA
-    lattice, local, pseudo = pl.pallas_call(
+    results = pl.pallas_call(
         functools.partial(kernel, n_hist, n_ka),
         out_shape=(
-            jax.ShapeDtypeStruct((block, orb, orb, 2, lanes), bf16),
-            jax.ShapeDtypeStruct((orb, orb, 2, block), f32),
-            jax.ShapeDtypeStruct((2, block, states), f32),
+            jax.ShapeDtypeStruct((rows, lanes), f32),
+            jax.ShapeDtypeStruct((8, lanes), f32),
+            jax.ShapeDtypeStruct((block, 2 * states), f32),
         ),
-        in_specs=[pl.BlockSpec(memory_space=pltpu.SMEM)] + [vmem] * 9,
+        in_specs=[pl.BlockSpec(memory_space=pltpu.SMEM)] + [vmem] * 2
+        + [pl.BlockSpec(memory_space=pl.ANY)] + [vmem] * 6,
         out_specs=(vmem, vmem, vmem),
         scratch_shapes=[
+            pltpu.VMEM(lattice_history.shape, bf16),
             pltpu.VMEM((block, orb, orb, 2, lanes), f32),
             pltpu.VMEM((orb * block, lanes), f32),
-            pltpu.VMEM((per_tile, sent_rows, lanes), f32),
-            pltpu.VMEM((n_hist, sent_rows, lanes), bf16),
-            pltpu.VMEM((n_hist, sent_rows, lanes), bf16),
+            pltpu.VMEM((per_tile, rows, lanes), f32),
+            pltpu.VMEM((8, lanes), f32),
+            pltpu.VMEM((n_hist, 8, lanes), f32),
+            pltpu.VMEM((n_hist, 1, lanes), f32),
+            pltpu.VMEM((n_hist, 1, lanes), f32),
+            pltpu.VMEM((n_hist, rows, lanes), bf16),
+            pltpu.VMEM((n_hist, rows, lanes), bf16),
             pltpu.VMEM((rows, lanes), f32),
             pltpu.VMEM((rows, lanes), f32),
             pltpu.VMEM((lanes, lanes), f32),
-            pltpu.VMEM((8, lanes), f32),
-            pltpu.VMEM((n_ka, 8, lanes), f32),
+            pltpu.VMEM((1, lanes), f32),
+            pltpu.VMEM((n_ka, 1, lanes), f32),
             pltpu.VMEM((block, 2, times, 2 * states), f32),
             pltpu.VMEM((n_hist, block, 2 * states), f32),
             pltpu.VMEM((n_hist, block, 2 * states), f32),
+            dma,
+            dma((n_hist,)),
+            dma((n_hist,)),
+            dma((n_hist,)),
+            dma((n_hist,)),
             dma((n_hist,)),
             dma((n_hist,)),
             dma((n_ka,)),
@@ -387,6 +434,16 @@
         jnp.transpose(predicted_row, (0, 2, 1)),
         jnp.transpose(pseudo_history, (0, 1, 3, 2)),
     )
+    lattice, local, pseudo = pl.pallas_call(
+        lay_out,
+        out_shape=(
+            jax.ShapeDtypeStruct((block, orb, orb, 2, lanes), bf16),
+            jax.ShapeDtypeStruct((orb, orb, 2, block), f32),
+            jax.ShapeDtypeStruct((2, block, states), f32),
+        ),
+        in_specs=[vmem] * 3,
+        out_specs=(vmem, vmem, vmem),
+    )(*results)
     return (
         jnp.transpose(lattice, (0, 3, 1, 2, 4)),
         jnp.transpose(local, (2, 0, 1, 3)),

time: 23 us -> 21.1 us (0.917)
  local copies, waits for them, and re-layouts: 2.63 us -> 0 us
  Pallas kernels: 18.8 us -> 19.5 us
    unnamed x7 -> x0, local copies, waits for them, and re-layouts: 2.63 us -> none
    pallas_call x0 -> x1, Pallas kernels: none -> 1.46 us  [per_device(): pl.pallas_call(lay_out, out_shape=(jax.ShapeDtypeStruct((block, orb, orb,...]
    pallas_call x1, Pallas kernels: 18.8 us -> 18.1 us  [per_device(): pl.pallas_call(functools.partial(kernel, n_hist, n_ka), out_shape=(jax.Sh...]
where the time goes in v3:
time: 21.1 us; the launch traced here: 20.8 us
  Pallas kernels  19.5 us (92%)
  between operations  1.29 us (6%)
    pallas_call x1, Pallas kernels, per_device(): pl.pallas_call(functools.partial(kernel, n_hist, n_ka), out_shape=(jax.Sh...  18.1 us
    pallas_call x1, Pallas kernels, per_device(): pl.pallas_call(lay_out, out_shape=(jax.ShapeDtypeStruct((block, orb, orb,...  1.46 us

profile of v3, /device:TPU:0, one launch (start us, length us, event | category | flops | bytes accessed | tf_op | source)
XLA Modules:
  0.0 20.8 jit_solution(2163133894285275208)
XLA Ops:
  1.3 18.1 %shard_map.121 = (f32[72,128]{1,0:T(8,128)}, f32[8,128]{1,0:T(8,128)}, f32[4,128]{1,0:T(4,128)}) custom-call(s32[1]{0:T(128)S(6)} %copy.13.step_ref, f32[3,4,128]{2,1,0:T(4,128)} %bitcast.14, bf16[4,3,3,2,128]{4,3,2,1,0:T(2,128)(2,1)} %bitcast.12, bf16[4,2,3,3,32,128]{5,4,3,2,1,0:T(8,128)(2,1)} %hist_ref.1, f32[3,3,2,128]{3,2,1,0:T(2,128)} %bitcast.13, ...), custom_call_target="tpu_custom_call" | custom-call | tf_op jit(solution)/shard_map/pallas_call | solution.py:383
  19.3 1.5 %shard_map.122 = (bf16[4,3,3,2,128]{4,3,2,1,0:T(2,128)(2,1)}, f32[3,3,2,4]{3,2,1,0:T(2,128)}, f32[2,4,64]{2,1,0:T(4,128)}) custom-call(f32[72,128]{1,0:T(8,128)} %get-tuple-element.9.total_ref, f32[8,128]{1,0:T(8,128)} %get-tuple-element.10.local_ref, f32[4,128]{1,0:T(4,128)} %get-tuple-element.11.pseudo_ref), custom_call_target="tpu_custom_call" | custom-call | tf_op jit(solution)/shard_map/pallas_call | solution.py:437

commit v4 on v3

--- a/solution.py
+++ b/solution.py
@@ -11,6 +11,12 @@
 coupling = 0.02
 tile_rows = 16
 highest = lax.Precision.HIGHEST
+
+
+def weighted_sums(mult, values):
+    upper = values.astype(jnp.bfloat16)
+    lower = (values - upper.astype(jnp.float32)).astype(jnp.bfloat16)
+    return dot_rows(mult, upper) + dot_rows(mult, lower)
 
 
 def dot_rows(left, right, precision=None):
@@ -27,6 +33,18 @@
     n_hist,
     n_ka,
     step_ref,
+    band_any,
+    krow_any,
+    hist_any,
+    dinv_any,
+    mult_any,
+    energy_any,
+    conn_any,
+    pred_any,
+    pseudo_any,
+    total_out,
+    local_out,
+    pseudo_out,
     band_ref,
     krow_ref,
     hist_ref,
@@ -36,10 +54,6 @@
     conn_ref,
     pred_ref,
     pseudo_ref,
-    total_out,
-    local_out,
-    pseudo_out,
-    hist_vmem,
     kw,
     suffix,
     stage,
@@ -57,7 +71,7 @@
     turned,
     qsend,
     qrecv,
-    hist_sem,
+    load_sem,
     esend_sem,
     erecv_sem,
     lsend_sem,
@@ -78,8 +92,6 @@
     me = lax.axis_index("hist")
     my_ka = lax.axis_index("ka")
 
-    load = pltpu.make_async_copy(hist_ref, hist_vmem, hist_sem)
-    load.start()
     barrier = pltpu.get_barrier_semaphore()
 
     def greet(hop, carry):
@@ -96,6 +108,19 @@
             device_id_type=pl.DeviceIdType.MESH,
         )
 
+    sources = (
+        krow_any, band_any, mult_any, hist_any, dinv_any, energy_any, conn_any, pred_any, pseudo_any
+    )
+    targets = (
+        krow_ref, band_ref, mult_ref, hist_ref, dinv_ref, energy_ref, conn_ref, pred_ref, pseudo_ref
+    )
+    loads = [
+        pltpu.make_async_copy(source, target, load_sem.at[i])
+        for i, (source, target) in enumerate(zip(sources, targets))
+    ]
+    for load in loads:
+        load.start()
+
     current = step_ref[0]
     first = me * block
     before = [jnp.where(first + m < current, 1.0, 0.0) for m in range(block)]
@@ -103,6 +128,8 @@
         jnp.where(first + m == 0, 0.5, 1.0) * before[m] for m in range(block)
     ]
 
+    for load in loads[:3]:
+        load.wait()
     for m in range(block):
         kw[m] = krow_ref[m].astype(jnp.float32) * weight[m]
 
@@ -113,7 +140,7 @@
             run = run + band_ref[c, m : m + 1, :] * before[m]
             suffix[c * block + m : c * block + m + 1, :] = run
         esend[c : c + 1, :] = run
-    mult = jnp.broadcast_to(mult_ref[...].astype(jnp.float32), (8, lanes))
+    mult = jnp.broadcast_to(mult_ref[...].astype(jnp.float32), (8, lanes)).astype(jnp.bfloat16)
 
     pl.semaphore_wait(barrier, n_hist - 1 + n_ka - 1)
 
@@ -144,7 +171,8 @@
         return carry
 
     lax.fori_loop(0, me, give_energy, 0)
-    load.wait()
+    for load in loads[3:]:
+        load.wait()
 
     def one_tile(tile, carry):
         at = pl.ds(pl.multiple_of(tile * tile_rows, tile_rows), tile_rows)
@@ -156,8 +184,8 @@
                 k_re = [kw[m, a, b, 0:1, :] for a in range(orb)]
                 k_im = [kw[m, a, b, 1:2, :] for a in range(orb)]
                 for c in range(orb):
-                    h_re = hist_vmem[m, 0, b, c, at, :].astype(jnp.float32)
-                    h_im = hist_vmem[m, 1, b, c, at, :].astype(jnp.float32)
+                    h_re = hist_ref[m, 0, b, c, at, :].astype(jnp.float32)
+                    h_im = hist_ref[m, 1, b, c, at, :].astype(jnp.float32)
                     for a in range(orb):
                         real[a][c] += k_re[a] * h_re - k_im[a] * h_im
                         imag[a][c] += k_re[a] * h_im + k_im[a] * h_re
@@ -173,9 +201,10 @@
                     row = ((s * orb + a) * orb + c) * block
                     for d in range(per_tile):
                         stage[d, row : row + block, :] = value[d * block : (d + 1) * block]
+        sums = weighted_sums(mult, stage[...].reshape(per_tile * rows, lanes))
         for d in range(per_tile):
             target = tile * per_tile + d
-            lsend[target, :, :rows] = dot_rows(mult, stage[d], highest)[:1]
+            lsend[target, :, :rows] = sums[:1, d * rows : (d + 1) * rows]
 
             @pl.when(target < me)
             def _():
@@ -258,7 +287,7 @@
     total[:half, :] = d_re * f_re - d_im * f_im
     total[half:rows, :] = d_re * f_im + d_im * f_re
 
-    free_sums = dot_rows(mult, total[...], highest)[:1]
+    free_sums = weighted_sums(mult, total[...])[:1]
 
     def take_sum(source, value):
         sum_copy(source, me).wait_recv()
@@ -380,6 +409,17 @@
     vmem = pl.BlockSpec(memory_space=pltpu.VMEM)
     f32, bf16 = jnp.float32, jnp.bfloat16
     dma = pltpu.SemaphoreType.DMA
+    operands = (
+        jnp.transpose(band_energy, (1, 0, 2)),
+        jnp.transpose(kernel_row, (0, 2, 3, 1, 4)),
+        lattice_history,
+        jnp.transpose(diagonal_inverse, (1, 2, 0, 3)),
+        multiplicity[None],
+        state_energy[None],
+        jnp.transpose(connection),
+        jnp.transpose(predicted_row, (0, 2, 1)),
+        jnp.transpose(pseudo_history, (0, 1, 3, 2)),
+    )
     results = pl.pallas_call(
         functools.partial(kernel, n_hist, n_ka),
         out_shape=(
@@ -387,11 +427,11 @@
             jax.ShapeDtypeStruct((8, lanes), f32),
             jax.ShapeDtypeStruct((block, 2 * states), f32),
         ),
-        in_specs=[pl.BlockSpec(memory_space=pltpu.SMEM)] + [vmem] * 2
-        + [pl.BlockSpec(memory_space=pl.ANY)] + [vmem] * 6,
+        in_specs=[pl.BlockSpec(memory_space=pltpu.SMEM)]
+        + [pl.BlockSpec(memory_space=pl.ANY)] * len(operands),
         out_specs=(vmem, vmem, vmem),
         scratch_shapes=[
-            pltpu.VMEM(lattice_history.shape, bf16),
+            *[pltpu.VMEM(array.shape, array.dtype) for array in operands],
             pltpu.VMEM((block, orb, orb, 2, lanes), f32),
             pltpu.VMEM((orb * block, lanes), f32),
             pltpu.VMEM((per_tile, rows, lanes), f32),
@@ -409,7 +449,7 @@
             pltpu.VMEM((block, 2, times, 2 * states), f32),
             pltpu.VMEM((n_hist, block, 2 * states), f32),
             pltpu.VMEM((n_hist, block, 2 * states), f32),
-            dma,
+            dma((len(operands),)),
             dma((n_hist,)),
             dma((n_hist,)),
             dma((n_hist,)),
@@ -424,15 +464,7 @@
         compiler_params=pltpu.CompilerParams(collective_id=0, has_side_effects=True),
     )(
         step_index,
-        jnp.transpose(band_energy, (1, 0, 2)),
-        jnp.transpose(kernel_row, (0, 2, 3, 1, 4)),
-        lattice_history,
-        jnp.transpose(diagonal_inverse, (1, 2, 0, 3)),
-        multiplicity[None],
-        state_energy[None],
-        jnp.transpose(connection),
-        jnp.transpose(predicted_row, (0, 2, 1)),
-        jnp.transpose(pseudo_history, (0, 1, 3, 2)),
+        *operands,
     )
     lattice, local, pseudo = pl.pallas_call(
         lay_out,

time: 21.1 us -> 19.6 us (0.929)
  Pallas kernels: 19.5 us -> 18.1 us
    pallas_call x1, Pallas kernels: 18.1 us -> 16.6 us  [per_device(): pl.pallas_call(functools.partial(kernel, n_hist, n_ka), out_shape=(jax.Sh...]
where the time goes in v4:
time: 19.6 us; the launch traced here: 19.4 us
  Pallas kernels  18.1 us (92%)
  between operations  1.29 us (7%)
    pallas_call x1, Pallas kernels, per_device(): pl.pallas_call(functools.partial(kernel, n_hist, n_ka), out_shape=(jax.Sh...  16.6 us
    pallas_call x1, Pallas kernels, per_device(): pl.pallas_call(lay_out, out_shape=(jax.ShapeDtypeStruct((block, orb, orb,...  1.46 us

profile of v4, /device:TPU:0, one launch (start us, length us, event | category | flops | bytes accessed | tf_op | source)
XLA Modules:
  0.0 19.4 jit_solution(5205755170521817173)
XLA Ops:
  1.3 16.6 %shard_map.121 = (f32[72,128]{1,0:T(8,128)}, f32[8,128]{1,0:T(8,128)}, f32[4,128]{1,0:T(4,128)}) custom-call(s32[1]{0:T(128)S(6)} %copy.13.step_ref, f32[3,4,128]{2,1,0:T(4,128)} %bitcast.14, bf16[4,3,3,2,128]{4,3,2,1,0:T(2,128)(2,1)} %bitcast.12, bf16[4,2,3,3,32,128]{5,4,3,2,1,0:T(8,128)(2,1)} %hist_any.1, f32[3,3,2,128]{3,2,1,0:T(2,128)} %bitcast.13, ...), custom_call_target="tpu_custom_call" | custom-call | tf_op jit(solution)/shard_map/pallas_call | solution.py:423
  17.9 1.5 %shard_map.122 = (bf16[4,3,3,2,128]{4,3,2,1,0:T(2,128)(2,1)}, f32[3,3,2,4]{3,2,1,0:T(2,128)}, f32[2,4,64]{2,1,0:T(4,128)}) custom-call(f32[72,128]{1,0:T(8,128)} %get-tuple-element.9.total_ref, f32[8,128]{1,0:T(8,128)} %get-tuple-element.10.local_ref, f32[4,128]{1,0:T(4,128)} %get-tuple-element.11.pseudo_ref), custom_call_target="tpu_custom_call" | custom-call | tf_op jit(solution)/shard_map/pallas_call | solution.py:469

commit v5 on v4

--- a/solution.py
+++ b/solution.py
@@ -230,6 +230,55 @@
                     dinv_ref[a, c, s : s + 1, :], (block, lanes)
                 )
     total[rows:, :] = jnp.ones((lanes - rows, lanes), jnp.float32)
+    def take_energy(source, later):
+        energy_copy(source, me).wait_recv()
+        return later + erecv[source]
+
+    later = lax.fori_loop(
+        me + 1, n_hist, take_energy, jnp.zeros(esend.shape, jnp.float32)
+    )
+    for c in range(orb):
+        for j in range(block):
+            frep[c * block + j : c * block + j + 1, :] = (
+                later[c : c + 1] + suffix[c * block + j : c * block + j + 1, :]
+            )
+    size = orb * block
+    angle = time_step * frep[:size, :]
+    when = first + lax.rem(lax.broadcasted_iota(jnp.int32, (size, lanes), 0), block)
+    inside = jnp.where(when <= current, 1.0, 0.0)
+    free_re = -jnp.sin(angle) * inside
+    free_im = -jnp.cos(angle) * inside
+    for a in range(orb):
+        frep[a * size : (a + 1) * size, :] = free_re
+        frep[(orb + a) * size : (orb + a + 1) * size, :] = free_im
+    half = rows // 2
+    f_re, f_im = frep[:half, :], frep[half:, :]
+    d_re, d_im = drep[:half, :], drep[half:, :]
+    total[:half, :] = d_re * f_re - d_im * f_im
+    total[half:rows, :] = d_re * f_im + d_im * f_re
+
+    free_sums = weighted_sums(mult, total[...])[:1]
+
+    def take_sum(source, value):
+        sum_copy(source, me).wait_recv()
+        return value + lrecv[source][:, :rows]
+
+    own_sums = lsend[me][:, :rows] + free_sums[:, :rows]
+    ksend[...] = free_sums
+    ksend[:, :rows] = lax.fori_loop(me + 1, n_hist, take_sum, own_sums)
+
+    def local_copy(source, target):
+        return pltpu.make_async_remote_copy(
+            src_ref=ksend,
+            dst_ref=krecv.at[source],
+            send_sem=ksend_sem.at[target],
+            recv_sem=krecv_sem.at[source],
+            device_id={"ka": target},
+            device_id_type=pl.DeviceIdType.MESH,
+        )
+
+    for hop in range(1, n_ka):
+        local_copy(my_ka, lax.rem(my_ka + hop, n_ka)).start()
     for m in range(block):
         h_re = pseudo_ref[m, 0].astype(jnp.float32)
         h_im = pseudo_ref[m, 1].astype(jnp.float32)
@@ -260,55 +309,6 @@
     free_pseudo = jnp.where(lane_of < states, -jnp.sin(spins), -jnp.cos(spins))
     free_pseudo = free_pseudo * jnp.where(row_time <= current, 1.0, 0.0)
 
-    def take_energy(source, later):
-        energy_copy(source, me).wait_recv()
-        return later + erecv[source]
-
-    later = lax.fori_loop(
-        me + 1, n_hist, take_energy, jnp.zeros(esend.shape, jnp.float32)
-    )
-    for c in range(orb):
-        for j in range(block):
-            frep[c * block + j : c * block + j + 1, :] = (
-                later[c : c + 1] + suffix[c * block + j : c * block + j + 1, :]
-            )
-    size = orb * block
-    angle = time_step * frep[:size, :]
-    when = first + lax.rem(lax.broadcasted_iota(jnp.int32, (size, lanes), 0), block)
-    inside = jnp.where(when <= current, 1.0, 0.0)
-    free_re = -jnp.sin(angle) * inside
-    free_im = -jnp.cos(angle) * inside
-    for a in range(orb):
-        frep[a * size : (a + 1) * size, :] = free_re
-        frep[(orb + a) * size : (orb + a + 1) * size, :] = free_im
-    half = rows // 2
-    f_re, f_im = frep[:half, :], frep[half:, :]
-    d_re, d_im = drep[:half, :], drep[half:, :]
-    total[:half, :] = d_re * f_re - d_im * f_im
-    total[half:rows, :] = d_re * f_im + d_im * f_re
-
-    free_sums = weighted_sums(mult, total[...])[:1]
-
-    def take_sum(source, value):
-        sum_copy(source, me).wait_recv()
-        return value + lrecv[source][:, :rows]
-
-    own_sums = lsend[me][:, :rows] + free_sums[:, :rows]
-    ksend[...] = free_sums
-    ksend[:, :rows] = lax.fori_loop(me + 1, n_hist, take_sum, own_sums)
-
-    def local_copy(source, target):
-        return pltpu.make_async_remote_copy(
-            src_ref=ksend,
-            dst_ref=krecv.at[source],
-            send_sem=ksend_sem.at[target],
-            recv_sem=krecv_sem.at[source],
-            device_id={"ka": target},
-            device_id_type=pl.DeviceIdType.MESH,
-        )
-
-    for hop in range(1, n_ka):
-        local_copy(my_ka, lax.rem(my_ka + hop, n_ka)).start()
     local = ksend[...]
     for hop in range(1, n_ka):
         source = lax.rem(my_ka + hop, n_ka)

time: 19.6 us -> 19.6 us (level)
  no operation moved by 1% of the time
where the time goes in v5:
time: 19.6 us; the launch traced here: 19.4 us
  Pallas kernels  18.1 us (92%)
  between operations  1.29 us (7%)
    pallas_call x1, Pallas kernels, per_device(): pl.pallas_call(functools.partial(kernel, n_hist, n_ka), out_shape=(jax.Sh...  16.6 us
    pallas_call x1, Pallas kernels, per_device(): pl.pallas_call(lay_out, out_shape=(jax.ShapeDtypeStruct((block, orb, orb,...  1.46 us

profile of v5, /device:TPU:0, one launch (start us, length us, event | category | flops | bytes accessed | tf_op | source)
XLA Modules:
  0.0 19.4 jit_solution(3533352281779985808)
XLA Ops:
  1.3 16.6 %shard_map.121 = (f32[72,128]{1,0:T(8,128)}, f32[8,128]{1,0:T(8,128)}, f32[4,128]{1,0:T(4,128)}) custom-call(s32[1]{0:T(128)S(6)} %copy.13.step_ref, f32[3,4,128]{2,1,0:T(4,128)} %bitcast.14, bf16[4,3,3,2,128]{4,3,2,1,0:T(2,128)(2,1)} %bitcast.12, bf16[4,2,3,3,32,128]{5,4,3,2,1,0:T(8,128)(2,1)} %hist_any.1, f32[3,3,2,128]{3,2,1,0:T(2,128)} %bitcast.13, ...), custom_call_target="tpu_custom_call" | custom-call | tf_op jit(solution)/shard_map/pallas_call | solution.py:423
  17.9 1.5 %shard_map.122 = (bf16[4,3,3,2,128]{4,3,2,1,0:T(2,128)(2,1)}, f32[3,3,2,4]{3,2,1,0:T(2,128)}, f32[2,4,64]{2,1,0:T(4,128)}) custom-call(f32[72,128]{1,0:T(8,128)} %get-tuple-element.9.total_ref, f32[8,128]{1,0:T(8,128)} %get-tuple-element.10.local_ref, f32[4,128]{1,0:T(4,128)} %get-tuple-element.11.pseudo_ref), custom_call_target="tpu_custom_call" | custom-call | tf_op jit(solution)/shard_map/pallas_call | solution.py:469
